TPU v7x, 512 devices: a whole 4x8x8 slice. The times are simulated.
512 devices in a mesh: row: 16 (over y, core), col: 32 (over z, x).
Axes of the slice: x: 4, y: 8, z: 8, core: 2. Of those that a mesh axis runs over, the one named last changes fastest.
Arguments:
- points: bfloat16 [128, 65536], P(None, ('row', 'col')), may hold values from -6 to 6
- inv_scale: float32 [128], replicated, may hold values from 0.07 to 0.22
- basis: bfloat16 [65536, 4096], P(('row', 'col')), may hold values from -0.25 to 0.25
- shrink: float32 [4096], replicated, may hold values from 0.02 to 1
- solution: float32 [33, 65536], P(None, ('row', 'col')), may hold values from -6 to 6
- residual: float32 [33, 65536], P(None, ('row', 'col')), may hold values from -6 to 6
- direction_prev: float32 [33, 65536], P(None, ('row', 'col')), may hold values from -6 to 6
- rz_prev: float32 [33], replicated, may hold values from 65536 to 262144
Outputs:
- solution_next: float32 [33, 65536], P(None, ('row', 'col'))
- residual_next: float32 [33, 65536], P(None, ('row', 'col'))
- direction: float32 [33, 65536], P(None, ('row', 'col'))
All inputs are finite; a program needn't handle non-finite values.
Results may differ from a plain program's by a relative error of at most 0.019.
Values may be sent and summed in bfloat16 or wider, within the bound.
A program may use at most 64 MiB of HBM per device.

v0:
```python
import jax
import jax.numpy as jnp
from jax import lax
from jax.sharding import PartitionSpec as P

noise_level = 0.25


def local(points, inv_scale, basis, shrink, solution, residual, direction_prev, rz_prev):
    scaled = (points * inv_scale[:, None]).astype(jnp.bfloat16)
    residual_bf = residual.astype(jnp.bfloat16)
    local_proj = jnp.dot(residual_bf, basis, preferred_element_type=jnp.float32)
    damping = shrink - 1.0
    projected = lax.psum(local_proj, ("row", "col"))
    correction = (damping[None, :] * projected).astype(jnp.bfloat16)
    precond = residual + jnp.dot(correction, basis.T, preferred_element_type=jnp.float32)
    precond_inner = lax.psum(jnp.sum(residual * precond, axis=1), ("row", "col"))
    direction = precond + (precond_inner / rz_prev)[:, None] * direction_prev
    direction_bf = direction.astype(jnp.bfloat16)
    row_points = lax.all_gather(scaled, "col", axis=1, tiled=True)
    row_sq = jnp.sum(jnp.square(row_points.astype(jnp.float32)), axis=0)
    rows_total = row_points.shape[1]
    width = min(1024, rows_total)
    direction_piece = lax.all_gather(direction_bf, "row", axis=1, tiled=True)
    column_pts = lax.all_gather(scaled, "row", axis=1, tiled=True)
    column_sq = jnp.sum(jnp.square(column_pts.astype(jnp.float32)), axis=0)
    results = []
    for offset in range(0, rows_total, width):
        rows = row_points[:, offset : offset + width]
        cross = lax.dot_general(
            column_pts, rows, (((0,), (0,)), ((), ())), preferred_element_type=jnp.float32
        )
        distance = jnp.maximum(
            column_sq[:, None] + row_sq[None, offset : offset + width] - 2.0 * cross, 0.0
        )
        tile = jnp.exp(-0.5 * distance).astype(jnp.bfloat16)
        results.append(jnp.dot(direction_piece, tile, preferred_element_type=jnp.float32))
    image_part = jnp.concatenate(results, axis=1)
    image = (
        lax.psum_scatter(
            image_part.astype(jnp.bfloat16), "col", scatter_dimension=1, tiled=True
        ).astype(jnp.float32)
        + noise_level * direction
    )
    curvature = lax.psum(jnp.sum(direction * image, axis=1), ("row", "col"))
    alpha = precond_inner / curvature
    solution_next = solution + alpha[:, None] * direction
    residual_next = residual - alpha[:, None] * image
    return (solution_next, residual_next, direction)


def solution(mesh):
    placed = (
        P(None, ("row", "col")),
        P(),
        P(("row", "col"), None),
        P(),
        P(None, ("row", "col")),
        P(None, ("row", "col")),
        P(None, ("row", "col")),
        P(),
    )
    return jax.shard_map(
        local,
        mesh=mesh,
        in_specs=placed,
        out_specs=(P(None, ("row", "col")), P(None, ("row", "col")), P(None, ("row", "col"))),
        check_vma=False,
    )
```

profile of v0, /device:TPU:1, one launch (start us, length us, event | category | flops | bytes accessed | tf_op | source)
XLA Modules:
  0.0 740.1 jit_solution(11344339179035116326)
XLA Ops:
  8.0 0.0 copy-start
  8.0 0.0 copy-start.4
  8.0 0.0 copy-start.8
  8.0 0.0 all-reduce.2.cloned.1.call-start
  8.1 1.2 copy-done
  9.2 1.9 fusion.17
  11.1 0.0 copy-start.7
  11.1 0.0 copy-start.3
  11.1 0.0 all-reduce.2.cloned.1.call-update
  11.1 0.0 all-gather.2.cloned.1.call-start
  11.2 0.0 copy-done.4
  11.2 0.0 copy-done.8
  11.2 0.7 multiply_convert_fusion.2
  11.9 0.0 all-gather.2.cloned.1.call-update
  11.9 0.0 reduce-scatter.4.cloned.1.call-start
  11.9 22.7 %all_gather.10 = bf16[128,2048]{1,0:T(8,128)(2,1)S(1)} all-gather(bf16[128,128]{1,0:T(8,128)(2,1)} %multiply_convert_fusion.2), channel_id=1, replica_groups=mesh['row'=16,'col'=32] {'row'}, dimensions={1}, use_global_device_ids=true | all-gather | bytes 557056 | tf_op jit(solution)/shard_map/all_gather | solution.py:25
  34.6 0.0 copy-start.9
  34.6 0.0 copy-start.6
  34.6 0.1 multiply_reduce_fusion.1
  34.8 0.0 copy-done.7
  34.8 256.8 %all-reduce.2.cloned.1.call-done = f32[33,4096]{1,0:T(8,128)} async-done(((f32[33,4096]{1,0:T(8,128)}), f32[33,4096]{1,0:T(8,128)}) %all-reduce.2.cloned.1.call-update) | async-done | bytes 540688 | tf_op jit(solution)/shard_map/psum | solution.py:14
  291.6 0.0 copy-done.3
  291.6 1.7 multiply_reduce_fusion.3
  293.3 97.0 %psum.22 = f32[33]{0:T(128)S(1)} all-reduce(f32[33]{0:T(128)S(1)} %get-tuple-element.11), channel_id=1, replica_groups=mesh['row'=16,'col'=32] {'row','col'}, use_global_device_ids=true, to_apply=%region_2.0 | all-reduce | flops 33 | bytes 264 | tf_op jit(solution)/shard_map/psum | solution.py:17
  390.3 0.0 copy-done.9
  390.3 0.0 copy-done.6
  390.3 0.1 fusion.31
  390.4 0.0 copy-start.2
  390.4 15.4 %all_gather.9 = bf16[33,2048]{1,0:T(8,128)(2,1)S(1)} all-gather(bf16[33,128]{1,0:T(8,128)(2,1)S(1)} %get-tuple-element.3), channel_id=1, replica_groups=mesh['row'=16,'col'=32] {'row'}, dimensions={1}, use_global_device_ids=true | all-gather | bytes 143616 | tf_op jit(solution)/shard_map/all_gather | solution.py:24
  405.7 0.0 all-gather.2.cloned.1.call-done
  405.7 0.0 copy-start.1
  405.7 1.5 multiply_reduce_fusion
  407.3 0.0 copy-done.1
  407.3 2.7 fusion.4
  410.0 2.7 fusion.5
  412.7 2.7 fusion.6
  415.5 2.7 fusion.7
  418.2 0.0 copy-start.5
  418.2 1.4 copy.11
  419.6 0.0 reduce-scatter.4.cloned.1.call-update
  419.7 210.6 %reduce-scatter.4.cloned.1.call-done = bf16[128,33]{1,0:T(8,128)(2,1)} async-done(((bf16[4096,33]{1,0:T(8,128)(2,1)}), bf16[128,33]{1,0:T(8,128)(2,1)}) %reduce-scatter.4.cloned.1.call-update) | async-done | bytes 8464
  630.3 0.8 copy.12
  631.1 0.1 multiply_reduce_fusion.2
  631.2 100.7 %psum.23 = f32[33]{0:T(128)S(1)} all-reduce(f32[33]{0:T(128)S(1)} %multiply_reduce_fusion.2), channel_id=1, replica_groups=mesh['row'=16,'col'=32] {'row','col'}, use_global_device_ids=true, to_apply=%region_7.0 | all-reduce | flops 33 | bytes 264 | tf_op jit(solution)/shard_map/psum | solution.py:45
  731.9 0.0 copy-done.2
  731.9 0.0 copy-done.5
  731.9 0.7 multiply_subtract_fusion
  (5 shorter events, 0.0 us)
Async XLA Ops:
  8.0 1.2 copy-start
  8.0 3.2 copy-start.4
  8.0 3.2 copy-start.8
  8.0 283.6 %all-reduce.2.cloned.1.call-start = ((), (), s32[]{:S(2)}) async-start(), calls=%async_computation.1 | async-start | bytes 1310720 | tf_op jit(solution)/shard_map/psum | solution.py:14
  11.1 23.7 %copy-start.7 = (f32[4096]{0:T(1024)S(1)}, f32[4096]{0:T(1024)}, u32[]{:S(2)}) copy-start(f32[4096]{0:T(1024)} %param.11) | copy-start | bytes 49156
  11.1 280.5 %copy-start.3 = (f32[33,128]{1,0:T(8,128)S(1)}, f32[33,128]{1,0:T(8,128)}, u32[]{:S(2)}) copy-start(f32[33,128]{1,0:T(8,128)} %param.13) | copy-start | bytes 50692
  11.1 394.6 %all-gather.2.cloned.1.call-start = ((), (), s32[]{:S(2)}) async-start(), calls=%async_computation.2 | async-start | bytes 1081344 | tf_op jit(solution)/shard_map/all_gather | solution.py:20
  11.9 618.4 %reduce-scatter.4.cloned.1.call-start = ((), (), s32[]{:S(2)}) async-start(), calls=%async_computation.3 | async-start | bytes 1081344
  34.6 355.6 %copy-start.9 = (f32[33]{0:T(128)S(1)}, f32[33]{0:T(128)}, u32[]{:S(2)}) copy-start(f32[33]{0:T(128)} %param.15) | copy-start | bytes 400
  34.6 355.6 %copy-start.6 = (f32[33,128]{1,0:T(8,128)S(1)}, f32[33,128]{1,0:T(8,128)}, u32[]{:S(2)}) copy-start(f32[33,128]{1,0:T(8,128)} %param.14) | copy-start | bytes 50692
  390.4 341.6 %copy-start.2 = (f32[33,128]{1,0:T(8,128)}, f32[33,128]{1,0:T(8,128)S(1)}, u32[]{:S(2)}) copy-start(f32[33,128]{1,0:T(8,128)S(1)} %get-tuple-element.4) | copy-start | bytes 50692
  405.7 1.6 copy-start.1
  418.2 313.7 %copy-start.5 = (f32[33,128]{1,0:T(8,128)S(1)}, f32[33,128]{1,0:T(8,128)}, u32[]{:S(2)}) copy-start(f32[33,128]{1,0:T(8,128)} %param.12) | copy-start | bytes 50692
Sparse Core Ops, SparseCore 0:
  13.8 277.7 all-reduce.1
Sparse Core Ops, SparseCore 1:
  15.1 78.6 all-gather.1
  419.7 210.5 reduce-scatter.3
where the time goes:
time: 740 us
  waiting for transfers between devices  467 us (63%)
  blocking collectives  236 us (32%)
  between operations  15.6 us (2%)
  matrix products  14.4 us (2%)
    psum x1, waiting for transfers between devices, local(): projected = lax.psum(local_proj, ('row', 'col'))  257 us
    unnamed x4, waiting for transfers between devices  211 us
    psum x1, blocking collectives, local(): curvature = lax.psum(jnp.sum(direction * image, axis=1), ('row', 'col'))  101 us
    psum x1, blocking collectives, local(): lax.psum(jnp.sum(residual * precond, axis=1), ('row', 'col'))  97 us
    all_gather x1, blocking collectives, local(): column_pts = lax.all_gather(scaled, 'row', axis=1, tiled=True)  22.7 us
    all_gather x1, blocking collectives, local(): direction_piece = lax.all_gather(direction_bf, 'row', axis=1, tiled=True)  15.4 us
  transfers between devices with their start and end apart: 3, of which 2 were waited for; matrix products, arithmetic and copies ran while one was open for 0% of the time, Pallas kernels for 0%

commit v1 on v0

--- a/solution.py
+++ b/solution.py
@@ -22,7 +22,24 @@
     rows_total = row_points.shape[1]
     width = min(1024, rows_total)
     direction_piece = lax.all_gather(direction_bf, "row", axis=1, tiled=True)
-    column_pts = lax.all_gather(scaled, "row", axis=1, tiled=True)
+
+    def sites_search(inp):
+        n_dev_all = lax.psum(1, "row")
+        by_rank = [(u, (u + 1) % n_dev_all) for u in range(n_dev_all)]
+        tray = [(u, (u - 1) % n_dev_all) for u in range(n_dev_all)]
+        formed, outcome_arr = ([inp], [inp])
+        for _ in range(n_dev_all // 2):
+            formed.append(lax.ppermute(formed[-1], "row", by_rank))
+        for _ in range((n_dev_all - 1) // 2):
+            outcome_arr.append(lax.ppermute(outcome_arr[-1], "row", tray))
+        arr_next = jnp.roll(
+            jnp.concatenate([*formed[::-1], *outcome_arr[1:]], axis=1),
+            (lax.axis_index("row") - n_dev_all // 2) * inp.shape[1],
+            axis=1,
+        )
+        return arr_next
+
+    column_pts = sites_search(scaled)
     column_sq = jnp.sum(jnp.square(column_pts.astype(jnp.float32)), axis=0)
     results = []
     for offset in range(0, rows_total, width):

time: 740 us -> 744 us (level)
  starting transfers between devices: 0.13 us -> 29.6 us
  blocking collectives: 236 us -> 213 us
    ppermute x0 -> x15, starting transfers between devices: none -> 29.5 us  [the longest x7 26.8 us: sites_search(): outcome_arr.append(lax.ppermute(outcome_arr[-1], 'row', tray))]
    all_gather x1 -> x0, blocking collectives: 22.7 us -> none  [local(): column_pts = lax.all_gather(scaled, 'row', axis=1, tiled=True)]
    psum x1, waiting for transfers between devices: 257 us -> 240 us  [local(): projected = lax.psum(local_proj, ('row', 'col'))]
    ppermute x0 -> x15, waiting for transfers between devices: none -> 10.4 us  [the longest x8 8.66 us: sites_search(): formed.append(lax.ppermute(formed[-1], 'row', by_rank))]
  transfers between devices with their start and end apart: 3 -> 18, of which waited for: 2 -> 16; matrix products, arithmetic and copies ran while one was open for 0% -> 0% of each run, Pallas kernels for 0% -> 0%
where the time goes in v1:
time: 744 us
  waiting for transfers between devices  462 us (62%)
  blocking collectives  213 us (29%)
  starting transfers between devices  29.6 us (4%)
  between operations  15.8 us (2%)
  matrix products  15.6 us (2%)
    psum x1, waiting for transfers between devices, local(): projected = lax.psum(local_proj, ('row', 'col'))  240 us
    unnamed x4, waiting for transfers between devices  211 us
    psum x1, blocking collectives, local(): curvature = lax.psum(jnp.sum(direction * image, axis=1), ('row', 'col'))  101 us
    psum x1, blocking collectives, local(): lax.psum(jnp.sum(residual * precond, axis=1), ('row', 'col'))  97 us
    ppermute x7, starting transfers between devices, sites_search(): outcome_arr.append(lax.ppermute(outcome_arr[-1], 'row', tray))  26.8 us
    all_gather x1, blocking collectives, local(): direction_piece = lax.all_gather(direction_bf, 'row', axis=1, tiled=True)  15.5 us
  transfers between devices with their start and end apart: 18, of which 16 were waited for; matrix products, arithmetic and copies ran while one was open for 0% of the time, Pallas kernels for 0%

profile of v1, /device:TPU:1, one launch (start us, length us, event | category | flops | bytes accessed | tf_op | source)
XLA Modules:
  0.0 743.9 jit_solution(16294866178107994062)
XLA Ops:
  8.0 0.0 all-reduce.2.cloned.1.call-start
  8.1 1.1 copy-done
  9.2 1.8 fusion.25
  11.1 0.0 all-gather.2.cloned.1.call-start
  11.2 0.1 multiply_convert_fusion.2
  11.3 2.7 collective-permute-start
  14.0 4.9 collective-permute-done
  18.9 3.8 collective-permute-start.8
  22.7 0.7 collective-permute-done.1
  23.4 0.2 collective-permute-done.8
  23.6 3.7 collective-permute-start.9
  27.3 0.7 collective-permute-done.2
  28.0 0.2 collective-permute-done.9
  28.1 3.7 collective-permute-start.10
  31.8 0.7 collective-permute-done.3
  32.5 0.2 collective-permute-done.10
  32.7 3.7 collective-permute-start.11
  36.4 0.7 collective-permute-done.4
  37.1 0.2 collective-permute-done.11
  37.2 3.7 collective-permute-start.12
  41.0 0.7 collective-permute-done.5
  41.7 0.0 reduce-scatter.4.cloned.1.call-start
  41.7 0.1 collective-permute-done.12
  41.8 4.0 collective-permute-start.13
  45.9 0.3 collective-permute-done.6
  46.2 0.5 collective-permute-done.13
  46.7 4.1 collective-permute-start.14
  51.0 0.1 constant_dynamic-update-slice_fusion.23
  51.2 0.5 collective-permute-done.14
  51.8 0.1 constant_dynamic-update-slice_fusion.7
  52.1 0.1 multiply_reduce_fusion.1
  52.2 240.4 %all-reduce.2.cloned.1.call-done = f32[33,4096]{1,0:T(8,128)} async-done(((f32[33,4096]{1,0:T(8,128)}), f32[33,4096]{1,0:T(8,128)}) %all-reduce.2.cloned.1.call-update) | async-done | bytes 540688 | tf_op jit(solution)/shard_map/psum | solution.py:14
  292.6 1.7 multiply_reduce_fusion.3
  294.3 97.0 %psum.22 = f32[33]{0:T(128)S(1)} all-reduce(f32[33]{0:T(128)S(1)} %get-tuple-element.11), channel_id=1, replica_groups=mesh['row'=16,'col'=32] {'row','col'}, use_global_device_ids=true, to_apply=%region_2.0 | all-reduce | flops 33 | bytes 264 | tf_op jit(solution)/shard_map/psum | solution.py:17
  391.3 0.1 fusion.47
  391.4 15.5 %all_gather.6 = bf16[33,2048]{1,0:T(8,128)(2,1)S(1)} all-gather(bf16[33,128]{1,0:T(8,128)(2,1)S(1)} %get-tuple-element.3), channel_id=1, replica_groups=mesh['row'=16,'col'=32] {'row'}, dimensions={1}, use_global_device_ids=true | all-gather | bytes 143616 | tf_op jit(solution)/shard_map/all_gather | solution.py:24
  406.9 1.5 multiply_reduce_fusion
  408.5 2.7 fusion.7
  411.2 2.7 fusion.6
  413.9 3.4 fusion.5
  417.3 3.3 fusion.4
  420.6 0.9 pad_maximum_fusion
  421.6 1.4 copy.11
  423.0 211.0 %reduce-scatter.4.cloned.1.call-done = bf16[128,33]{1,0:T(8,128)(2,1)} async-done(((bf16[4096,33]{1,0:T(8,128)(2,1)}), bf16[128,33]{1,0:T(8,128)(2,1)}) %reduce-scatter.4.cloned.1.call-update) | async-done | bytes 8464
  634.1 0.8 copy.12
  634.9 0.1 multiply_reduce_fusion.2
  635.0 100.7 %psum.23 = f32[33]{0:T(128)S(1)} all-reduce(f32[33]{0:T(128)S(1)} %multiply_reduce_fusion.2), channel_id=1, replica_groups=mesh['row'=16,'col'=32] {'row','col'}, use_global_device_ids=true, to_apply=%region_7.8 | all-reduce | flops 33 | bytes 264 | tf_op jit(solution)/shard_map/psum | solution.py:62
  735.7 0.7 multiply_subtract_fusion
  (67 shorter events, 0.5 us)
Async XLA Ops:
  8.0 1.2 copy-start
  8.0 3.1 copy-start.2
  8.0 3.1 copy-start.9
  8.0 38.2 %copy-start.8 = (f32[4096]{0:T(1024)S(1)}, f32[4096]{0:T(1024)}, u32[]{:S(2)}) copy-start(f32[4096]{0:T(1024)} %param.11) | copy-start | bytes 49156
  8.0 284.6 %all-reduce.2.cloned.1.call-start = ((), (), s32[]{:S(2)}) async-start(), calls=%async_computation.1 | async-start | bytes 1310720 | tf_op jit(solution)/shard_map/psum | solution.py:14
  11.1 395.8 %all-gather.2.cloned.1.call-start = ((), (), s32[]{:S(2)}) async-start(), calls=%async_computation.2 | async-start | bytes 1081344 | tf_op jit(solution)/shard_map/all_gather | solution.py:20
  11.3 30.4 %copy-start.5 = (bf16[128,128]{1,0:T(8,128)(2,1)}, bf16[128,128]{1,0:T(8,128)(2,1)S(1)}, u32[]{:S(2)}) copy-start(bf16[128,128]{1,0:T(8,128)(2,1)S(1)} %multiply_convert_fusion.2) | copy-start | bytes 98308
  11.3 7.6 %collective-permute-start = (bf16[128,128]{1,0:T(8,128)(2,1)S(1)}, bf16[128,128]{1,0:T(8,128)(2,1)S(1)}, u32[]{:S(2)}, u32[]{:S(2)}) collective-permute-start(bf16[128,128]{1,0:T(8,128)(2,1)S(1)} %multiply_convert_fusion.2), channel_id=1, source_target_pairs={{0,32},{32,64},{64,96},{96,128},{128,160},{160,192},{192,224},{224... | collective-permute-start | bytes 98312 | tf_op jit(solution)/shard_map/ppermute | solution.py:32
  18.9 4.5 collective-permute-start.1
  18.9 4.7 collective-permute-start.8
  23.4 4.6 collective-permute-start.2
  23.6 4.6 collective-permute-start.9
  28.0 4.6 collective-permute-start.3
  28.1 4.6 collective-permute-start.10
  32.5 4.6 collective-permute-start.4
  32.7 4.6 collective-permute-start.11
  37.1 4.6 collective-permute-start.5
  37.2 4.6 collective-permute-start.12
  41.6 4.6 collective-permute-start.6
  41.7 592.4 %reduce-scatter.4.cloned.1.call-start = ((), (), s32[]{:S(2)}) async-start(), calls=%async_computation.3 | async-start | bytes 1081344
  41.8 4.9 collective-permute-start.13
  46.2 4.6 collective-permute-start.7
  46.7 4.9 collective-permute-start.14
  51.0 241.6 %copy-start.4 = (f32[33,128]{1,0:T(8,128)S(1)}, f32[33,128]{1,0:T(8,128)}, u32[]{:S(2)}) copy-start(f32[33,128]{1,0:T(8,128)} %param.13) | copy-start | bytes 50692
  52.1 339.2 %copy-start.10 = (f32[33]{0:T(128)S(1)}, f32[33]{0:T(128)}, u32[]{:S(2)}) copy-start(f32[33]{0:T(128)} %param.15) | copy-start | bytes 400
  52.1 339.2 %copy-start.7 = (f32[33,128]{1,0:T(8,128)S(1)}, f32[33,128]{1,0:T(8,128)}, u32[]{:S(2)}) copy-start(f32[33,128]{1,0:T(8,128)} %param.14) | copy-start | bytes 50692
  391.4 344.4 %copy-start.3 = (f32[33,128]{1,0:T(8,128)}, f32[33,128]{1,0:T(8,128)S(1)}, u32[]{:S(2)}) copy-start(f32[33,128]{1,0:T(8,128)S(1)} %get-tuple-element.4) | copy-start | bytes 50692
  406.9 1.6 copy-start.1
  421.6 314.1 %copy-start.6 = (f32[33,128]{1,0:T(8,128)S(1)}, f32[33,128]{1,0:T(8,128)}, u32[]{:S(2)}) copy-start(f32[33,128]{1,0:T(8,128)} %param.12) | copy-start | bytes 50692
Sparse Core Ops, SparseCore 0:
  13.8 278.7 all-reduce.1
Sparse Core Ops, SparseCore 1:
  41.8 76.3 all-gather.1
  423.1 210.9 reduce-scatter.3
